TPU v7x, 128 devices: a whole 4x4x4 slice. The times are simulated.
128 devices in a mesh: row: 8 (over z, core), col: 16 (over x, y).
Axes of the slice: x: 4, y: 4, z: 4, core: 2. Of those that a mesh axis runs over, the one named last changes fastest.
Arguments:
- offsets: float32 [8, 16, 2, 256], P('row', 'col'), may hold values from 0 to 1
- point_order: int32 [8, 16, 256], P('row', 'col'), may hold values from 0 to 255, each once within a row
- nugget: float32 [8, 16, 256], P('row', 'col'), may hold values from 1 to 4
- interp: float32 [8, 16, 128, 128], P('row', 'col'), may hold values from -0.5 to 0.5
Outputs:
- root_work: float32 [16384, 16384], P('row', 'col')
Inputs may be any that keep to these rules, and one draw needn't show every extreme that they name: `point_order`: each row lists every point of its box once; its first 128 entries name the box's skeleton points.
All inputs are finite; a program needn't handle non-finite values.
Results may differ from a plain program's by a relative error of at most 0.0001.
Values sent between devices are 32-bit elements; how exact they have to be, the bound alone decides.
A program may use at most 128 MiB of HBM per device.

v0:
```python
import jax
import jax.numpy as jnp
from jax import lax
from jax.sharding import PartitionSpec as P

PW = 512
kernel_amp = 0.015625
kernel_len = 0.5
highest = lax.Precision.HIGHEST


def extended(block, sides, width):
    for axis, dim in sides:
        count = lax.axis_size(axis)
        forward = [(i, i + 1) for i in range(count - 1)]
        backward = [(target, source) for source, target in forward]
        low = lax.ppermute(
            lax.slice_in_dim(block, block.shape[dim] - width, None, axis=dim), axis, forward
        )
        high = lax.ppermute(lax.slice_in_dim(block, 0, width, axis=dim), axis, backward)
        block = jnp.concatenate([low, block, high], axis=dim)
    return block


def shifted(block, axis, distance):
    devices = range(lax.axis_size(axis))
    route = [(i - distance, i) for i in devices if i - distance in devices]
    return lax.ppermute(block, axis, route)


def spread_2(value, axis, source):
    kept = jnp.where(lax.axis_index(axis) == source, value, 0).astype(value.dtype)
    return lax.psum(kept, axis)


def offsets_all():
    return [(a, b) for a in (-1, 0, 1) for b in (-1, 0, 1)]


def pairs_all():
    return [
        (e, m)
        for e in offsets_all()
        for m in offsets_all()
        if abs(m[0] - e[0]) <= 1 and abs(m[1] - e[1]) <= 1
    ]


def block_of(a, b):
    return (a + 1) * 3 + (b + 1)


def vector(along, across):
    return (along, across)


def kernel(left, right):
    gap_row = left[0][:, None] - right[0][None, :]
    gap_col = left[1][:, None] - right[1][None, :]
    return kernel_amp * jnp.exp(-jnp.sqrt(gap_row * gap_row + gap_col * gap_col) / kernel_len)


def cross_pair(stored, target, columns):
    pair_index = {pair: n for n, pair in enumerate(pairs_all())}
    left_rows = []
    right_rows = []
    for e in offsets_all():
        if abs(target[0] - e[0]) <= 1 and abs(target[1] - e[1]) <= 1:
            left_rows.append(stored[pair_index[e, (0, 0)]][:, :columns])
            right_rows.append(stored[pair_index[e, target]][:, :columns])
    return (jnp.concatenate(left_rows, axis=0), jnp.concatenate(right_rows, axis=0))


def cross_sum(stored, target, columns):
    left_rows, right_rows = cross_pair(stored, target, columns)
    return jnp.einsum("rk,rl->kl", left_rows, right_rows, precision=highest)


def eliminate(stored, near_matrix, interp_box):
    box_points = near_matrix.shape[0]
    skel_count = interp_box.shape[0]
    fill_blocks = [cross_sum(stored, m, box_points) for m in offsets_all()]
    matrix = near_matrix - jnp.concatenate(fill_blocks, axis=1)
    reduced_rows = matrix[skel_count:] - jnp.einsum(
        "sr,sk->rk", interp_box, matrix[:skel_count], precision=highest
    )
    centre = reduced_rows[:, 4 * box_points : 5 * box_points]
    reduced = centre[:, skel_count:] - jnp.einsum(
        "rs,st->rt", centre[:, :skel_count], interp_box, precision=highest
    )
    diag_factor = jnp.linalg.cholesky(reduced)
    return jax.scipy.linalg.solve_triangular(diag_factor, reduced_rows, lower=True)


def spread(factor_new, move_first, move_second, p):
    box_points = factor_new.shape[1] // 9

    def take_block(m):
        k = block_of(m[0], m[1])
        return factor_new[:, k * box_points : (k + 1) * box_points]

    placed = {}
    section_one = {}
    for s in (1, -1):
        listing = [vector(u, v) for u in (0, s) for v in (-1, 0, 1)]
        arrived = move_first(jnp.stack([take_block(m) for m in listing]), s)
        source = vector(-s, 0)
        section_one[s] = (source, listing, arrived)
        for n, m in enumerate(listing):
            placed[source, (m[0] + source[0], m[1] + source[1])] = arrived[n]
    for t in (1, -1):
        payload = []
        labels = []
        for m in [vector(u, v) for u in (-1, 0, 1) for v in (0, t)]:
            payload.append(take_block(m))
            labels.append(((0, 0), m))
        for s in (1, -1):
            source, listing, arrived = section_one[s]
            for n, m in enumerate(listing):
                if m[1 - p] in (0, t):
                    payload.append(arrived[n])
                    labels.append((source, m))
        arrived = move_second(jnp.stack(payload), t)
        sender_at = vector(0, -t)
        for n, (anchor, m) in enumerate(labels):
            source = (anchor[0] + sender_at[0], anchor[1] + sender_at[1])
            placed[source, (m[0] + source[0], m[1] + source[1])] = arrived[n]
    for m in offsets_all():
        placed[(0, 0), m] = take_block(m)
    return jnp.stack([placed[pair] for pair in pairs_all()])


def on_device(offsets, point_order, nugget, interp):
    row_at = lax.axis_index("row")
    col_at = lax.axis_index("col")
    row_count = lax.axis_size("row")
    col_count = lax.axis_size("col")
    box_points = offsets.shape[3]
    skel_count = interp.shape[2]
    red_count = interp.shape[3]
    corner = jnp.stack([row_at, col_at]).astype(jnp.float32)[:, None]
    points = jnp.take(offsets[0, 0] + corner, point_order[0, 0], axis=1)
    weights = jnp.take(nugget[0, 0], point_order[0, 0])
    interp_box = interp[0, 0]
    neighbour_points = extended(points[None, None], (("row", 0), ("col", 1)), 1)
    present = []
    kernel_blocks = []
    for a, b in offsets_all():
        inside = (
            (row_at + a >= 0)
            & (row_at + a < row_count)
            & (col_at + b >= 0)
            & (col_at + b < col_count)
        )
        present.append(inside.astype(jnp.float32))
        kernel_block = kernel(points, neighbour_points[a + 1, b + 1]) * present[-1]
        if (a, b) == (0, 0):
            kernel_block = kernel_block + jnp.diag(weights)
        kernel_blocks.append(kernel_block)
    near_matrix = jnp.concatenate(kernel_blocks, axis=1)

    def move_first(x, amount):
        return shifted(x, "row", amount)

    def move_second(x, amount):
        return shifted(x, "col", amount)

    leading = 0
    colour = 2 * (row_at % 2) + col_at % 2
    stored = jnp.zeros((len(pairs_all()), red_count, box_points), jnp.float32)
    for k in range(4):
        factor_new = lax.cond(
            colour == k,
            lambda s: eliminate(s, near_matrix, interp_box),
            lambda s: jnp.zeros((red_count, 9 * box_points), jnp.float32),
            stored,
        )
        stored = stored + spread(factor_new, move_first, move_second, leading)
    row_width = skel_count // row_count
    col_width = skel_count // col_count
    box_total = row_count * col_count
    weights_skel = weights[:skel_count]
    row_ids = jnp.arange(skel_count, dtype=jnp.int32).reshape(row_count, row_width)
    col_ids = jnp.arange(skel_count, dtype=jnp.int32).reshape(col_count, col_width)
    diag_piece = jnp.where(
        row_ids[:, None, :, None] == col_ids[None, :, None, :],
        weights_skel.reshape(row_count, row_width)[:, None, :, None],
        0.0,
    )
    pieces = []
    for k, m in enumerate(offsets_all()):
        left_rows, right_rows = cross_pair(stored, m, skel_count)
        fill_part = jnp.einsum(
            "rak,rbl->abkl",
            left_rows.reshape(-1, row_count, row_width),
            right_rows.reshape(-1, col_count, col_width),
            precision=highest,
        )
        if m == (0, 0):
            delta_block = diag_piece - fill_part
        else:
            delta_block = -fill_part
        pieces.append(delta_block * present[k])
    outgoing = jnp.stack(pieces, axis=2).reshape(box_total * 9, row_width * col_width)
    arrived = lax.all_to_all(outgoing, ("row", "col"), split_axis=0, concat_axis=0, tiled=True)
    received = jnp.transpose(arrived.reshape(box_total, 9, row_width, col_width), (1, 2, 0, 3))
    box_ids = jnp.arange(box_total, dtype=jnp.int32)
    src_rows = (box_ids // col_count)[:, None]
    src_cols = (box_ids % col_count)[:, None]
    all_skeleton = lax.all_gather(points[:, :skel_count][None], ("row", "col"), axis=0, tiled=True)
    row_part = lax.dynamic_slice_in_dim(all_skeleton, row_at * row_width, row_width, 2)
    col_part = lax.dynamic_slice_in_dim(all_skeleton, col_at * col_width, col_width, 2)
    row_coords = jnp.transpose(row_part, (1, 2, 0)).reshape(2, row_width * box_total)
    col_coords = jnp.transpose(col_part, (1, 2, 0)).reshape(2, col_width * box_total)
    placed = jnp.zeros((row_width, box_total, col_width, box_total), jnp.float32)
    for n, (a, b) in enumerate(offsets_all()):
        target = (src_rows + a) * col_count + src_cols + b
        living = (
            (src_rows + a >= 0)
            & (src_rows + a < row_count)
            & (src_cols + b >= 0)
            & (src_cols + b < col_count)
        )
        hit = (target == box_ids[None, :]) & living
        placed = jnp.where(hit[None, :, None, :], received[n][:, :, :, None], placed)
    delta_tile = placed.reshape(row_width * box_total, col_width * box_total)
    root_matrix = kernel(row_coords, col_coords) + delta_tile
    rows_here = root_matrix.shape[0]
    cols_here = root_matrix.shape[1]
    global_rows = row_at * rows_here + jnp.arange(rows_here, dtype=jnp.int32)
    global_cols = col_at * cols_here + jnp.arange(cols_here, dtype=jnp.int32)
    columns_out = []
    for p in range(2):
        first_col = p * PW
        owner_col = first_col // cols_here
        local_col = first_col % cols_here
        owner_row = first_col // rows_here
        local_row = first_col % rows_here
        own_slab = root_matrix[:, local_col : local_col + PW]
        slab_rows = spread_2(own_slab, "col", owner_col)
        diag_block = spread_2(slab_rows[local_row : local_row + PW], "row", owner_row)
        diag_factor = jnp.linalg.cholesky(diag_block)
        solved = jax.scipy.linalg.solve_triangular(diag_factor, slab_rows.T, lower=True).T
        pasted = lax.dynamic_update_slice(solved, diag_factor, (first_col - row_at * rows_here, 0))
        inside = (global_rows >= first_col) & (global_rows < first_col + PW)
        panel_rows = jnp.where(
            (global_rows < first_col)[:, None], 0.0, jnp.where(inside[:, None], pasted, solved)
        )
        first_global = col_at * cols_here
        holder = first_global // rows_here
        offset_rows = first_global - holder * rows_here
        panel_cols = spread_2(
            lax.dynamic_slice_in_dim(panel_rows, offset_rows, cols_here, 0), "row", holder
        )
        root_matrix = root_matrix - jnp.einsum(
            "rk,ck->rc", panel_rows, panel_cols, precision=highest
        )
        columns_out.append((owner_col, local_col, panel_rows))
    for owner_col, local_col, panel_rows in columns_out:
        current = root_matrix[:, local_col : local_col + PW]
        root_matrix = lax.dynamic_update_slice(
            root_matrix, jnp.where(col_at == owner_col, panel_rows, current), (0, local_col)
        )
    top_rows = min(2 * PW, rows_here)
    top_block = root_matrix[:top_rows]
    zero_mask = (global_rows[:top_rows, None] < 2 * PW) & (global_cols[None, :] >= 2 * PW)
    return lax.dynamic_update_slice(root_matrix, jnp.where(zero_mask, 0.0, top_block), (0, 0))


def solution(mesh):
    in_specs = (
        P("row", "col", None, None),
        P("row", "col", None),
        P("row", "col", None),
        P("row", "col", None, None),
    )
    out_specs = P("row", "col")
    return jax.shard_map(
        on_device, mesh=mesh, in_specs=in_specs, out_specs=out_specs, check_vma=False
    )
```

profile of v0, /device:TPU:0, one launch (start us, length us, event | category | flops | bytes accessed | tf_op | source)
XLA Modules:
  0.0 1654.9 jit_solution(10580641799856505549)
XLA Ops:
  14.9 3.6 collective-permute-done.1
  18.5 3.5 collective-permute-start.2
  24.2 3.3 collective-permute-done.3
  29.1 55.5 %conditional.4 = (f32[128,256]{1,0:T(8,128)}, f32[128,256]{1,0:T(8,128)}, f32[128,256]{1,0:T(8,128)}, f32[128,256]{1,0:T(8,128)}, f32[128,256]{1,0:T(8,128)}, /*...) conditional(s32[]{:T(128)} %convert_element_type.56, () %tuple.65, ...), branch_computations={%region_0.1_spmd, %region_1.6_spmd} | conditional | flops 2442133504 | bytes 22315710 | solution.py:172
  39.8 13.2 cholesky.356
  56.6 11.3 custom-call.35
  86.0 2.9 copy.446
  109.8 4.6 collective-permute-done.5
  119.9 29.2 %collective-permute-done.6 = f32[14,128,256]{2,1,0:T(8,128)} collective-permute-done((f32[14,128,256]{2,1,0:T(8,128)}, f32[14,128,256]{2,1,0:T(8,128)}, u32[]{:S(2)}, u32[]{:S(2)}) %collective-permute-start.6) | collective-permute-done | bytes 1835040 | tf_op jit(solution)/shard_map/ppermute | solution.py:28
  151.4 3.5 collective-permute-done.7
  168.6 8.2 conditional.5
  185.9 10.8 collective-permute-start.8
  201.8 7.9 collective-permute-done.9
  209.8 57.6 %collective-permute-start.10 = (f32[14,128,256]{2,1,0:T(8,128)S(1)}, f32[14,128,256]{2,1,0:T(8,128)S(1)}, u32[]{:S(2)}, u32[]{:S(2)}) collective-permute-start(f32[14,128,256]{2,1,0:T(8,128)S(1)} %get-tuple-element.880), channel_id=1, source_target_pairs={{0,1},{1,2},{2,3},{3,4},{4,5},{5,6},{6,7},{7,8},{8,9},{9,10},{10,1... | collective-permute-start | bytes 5505032 | tf_op jit(solution)/shard_map/ppermute | solution.py:28
  274.5 24.2 %collective-permute-done.10 = f32[14,128,256]{2,1,0:T(8,128)S(1)} collective-permute-done((f32[14,128,256]{2,1,0:T(8,128)S(1)}, f32[14,128,256]{2,1,0:T(8,128)S(1)}, u32[]{:S(2)}, u32[]{:S(2)}) %collective-permute-start.10) | collective-permute-done | bytes 1835040 | tf_op jit(solution)/shard_map/ppermute | solution.py:28
  298.8 5.6 collective-permute-done.11
  311.3 3.7 add.655
  315.1 9.1 conditional.6
  325.8 3.0 copy.582
  343.4 70.5 %collective-permute-start.12 = (f32[6,128,256]{2,1,0:T(8,128)S(1)}, f32[6,128,256]{2,1,0:T(8,128)S(1)}, u32[]{:S(2)}, u32[]{:S(2)}) collective-permute-start(f32[6,128,256]{2,1,0:T(8,128)S(1)} %get-tuple-element.968), channel_id=1, source_target_pairs={{0,16},{16,32},{32,48},{48,64},{64,80},{80,96},{96,112},{1,17},{17... | collective-permute-start | bytes 2359304 | tf_op jit(solution)/shard_map/ppermute | solution.py:28
  427.8 106.3 %all-gather.1 = f32[128,2,128]{2,1,0:T(2,128)S(1)} all-gather(f32[1,2,128]{2,1,0:T(2,128)S(1)} %copy.132), channel_id=2, replica_groups=mesh['row'=8,'col'=16] {'row','col'}, dimensions={0}, use_global_device_ids=true | all-gather | bytes 132096 | tf_op jit(solution)/shard_map/all_gather | solution.py:210
  560.8 6.9 add.656
  567.7 10.7 conditional.7
  597.4 51.3 %collective-permute-start.18 = (f32[14,128,256]{2,1,0:T(8,128)}, f32[14,128,256]{2,1,0:T(8,128)}, u32[]{:S(2)}, u32[]{:S(2)}) collective-permute-start(f32[14,128,256]{2,1,0:T(8,128)} %get-tuple-element.864), channel_id=1, source_target_pairs={{0,1},{1,2},{2,3},{3,4},{4,5},{5,6},{6,7},{7,8},{8,9},{9,10},{10,1... | collective-permute-start | bytes 5505032 | tf_op jit(solution)/shard_map/ppermute | solution.py:28
  661.2 18.5 %collective-permute-done.18 = f32[14,128,256]{2,1,0:T(8,128)} collective-permute-done((f32[14,128,256]{2,1,0:T(8,128)}, f32[14,128,256]{2,1,0:T(8,128)}, u32[]{:S(2)}, u32[]{:S(2)}) %collective-permute-start.18) | collective-permute-done | bytes 1835040 | tf_op jit(solution)/shard_map/ppermute | solution.py:28
  680.9 8.0 collective-permute-done.19
  693.5 4.1 add.657
  730.9 3.6 fusion.239
  755.3 20.8 %all-to-all-start = ((f32[128,9,128]{2,1,0:T(8,128)}), f32[128,9,128]{2,1,0:T(8,128)S(1)}, u32[]{:S(2)}, u32[]{:S(2)}) async-start(f32[128,9,128]{2,1,0:T(8,128)} %copy.165), calls=%async_computation | async-start | bytes 2097152 | tf_op jit(solution)/shard_map/all_to_all | solution.py:205
  776.4 18.7 %all-to-all-done = f32[128,9,128]{2,1,0:T(8,128)S(1)} async-done(((f32[128,9,128]{2,1,0:T(8,128)}), f32[128,9,128]{2,1,0:T(8,128)S(1)}, u32[]{:S(2)}, u32[]{:S(2)}) %all-to-all-start) | async-done | bytes 589856 | tf_op jit(solution)/shard_map/all_to_all | solution.py:205
  795.8 5.4 select_select_fusion.4
  801.2 6.1 bitcast_add_fusion.4
  807.3 3.4 copy-done.2
  813.4 98.8 %all-reduce.10.cloned.1.call-done = f32[2048,512]{0,1:T(8,128)} async-done(((f32[2048,512]{0,1:T(8,128)}), f32[2048,512]{0,1:T(8,128)}) %all-reduce.10.cloned.1.call-update) | async-done | bytes 4194320 | tf_op jit(solution)/shard_map/psum | solution.py:33
  915.0 62.4 %all-reduce.12.cloned.1.call-done = f32[512,512]{0,1:T(8,128)} async-done(((f32[512,512]{0,1:T(8,128)}), f32[512,512]{0,1:T(8,128)}) %all-reduce.12.cloned.1.call-update) | async-done | bytes 1048592 | tf_op jit(solution)/shard_map/psum | solution.py:33
  979.3 11.7 cholesky.402
  991.0 9.8 custom-call.39
  1001.5 11.7 cholesky.421
  1013.6 10.3 custom-call.40
  1024.9 11.7 cholesky.442
  1036.8 9.8 custom-call.41
  1047.4 11.9 cholesky.459
  1064.7 8.2 while.4
  1072.8 39.3 %custom-call.42 = f32[4,128,128]{1,2,0:T(8,128)S(1)} custom-call(f32[4,128,128]{2,1,0:T(8,128)S(1)} %get-tuple-element.489), custom_call_target="InvertDiagBlocksLowerTriangular" | custom-call | tf_op jit(solution)/shard_map/jit(_solve_triangular)/triangular_solve | solution.py:243
  1130.4 65.2 %all-reduce.14.cloned.1.call-done = f32[1024,512]{0,1:T(8,128)} async-done(((f32[1024,512]{0,1:T(8,128)}), f32[1024,512]{0,1:T(8,128)}) %all-reduce.14.cloned.1.call-update) | async-done | bytes 2097168 | tf_op jit(solution)/shard_map/psum | solution.py:33
  1195.6 17.6 %convolution_subtract_fusion.5 = f32[2048,1024]{0,1:T(8,128)S(1)} fusion(f32[2048,1024]{0,1:T(8,128)} %copy-done.2, f32[2048,512]{0,1:T(8,128)} %copy-done.9, f32[1024,512]{0,1:T(8,128)} %all-reduce.14.cloned.1.call-done), kind=kOutput, calls=%fused_computation.563 | convolution fusion | flops 12886999040 | bytes 23068672 | tf_op jit(solution)/shard_map/rk,ck->rc/dot_general | solution.py:255
  1213.2 3.4 copy-done.3
  1219.0 102.7 %all-reduce.16.cloned.1.call-done = f32[2048,512]{0,1:T(8,128)} async-done(((f32[2048,512]{0,1:T(8,128)}), f32[2048,512]{0,1:T(8,128)}) %all-reduce.16.cloned.1.call-update) | async-done | bytes 4194320 | tf_op jit(solution)/shard_map/psum | solution.py:33
  1324.1 62.7 %all-reduce.18.cloned.1.call-done = f32[512,512]{0,1:T(8,128)} async-done(((f32[512,512]{0,1:T(8,128)}), f32[512,512]{0,1:T(8,128)}) %all-reduce.18.cloned.1.call-update) | async-done | bytes 1048592 | tf_op jit(solution)/shard_map/psum | solution.py:33
  1388.8 11.7 cholesky.474
  1400.5 9.8 custom-call.43
  1411.0 11.7 cholesky.493
  1423.1 10.0 custom-call.44
  1434.1 11.7 cholesky.514
  1446.0 9.8 custom-call.45
  1456.6 11.9 cholesky.531
  1473.9 8.3 while.5
  1482.2 39.3 %custom-call.46 = f32[4,128,128]{1,2,0:T(8,128)S(1)} custom-call(f32[4,128,128]{2,1,0:T(8,128)S(1)} %get-tuple-element.490), custom_call_target="InvertDiagBlocksLowerTriangular" | custom-call | tf_op jit(solution)/shard_map/jit(_solve_triangular)/triangular_solve | solution.py:243
  1539.7 65.4 %all-reduce.20.cloned.1.call-done = f32[1024,512]{0,1:T(8,128)} async-done(((f32[1024,512]{0,1:T(8,128)}), f32[1024,512]{0,1:T(8,128)}) %all-reduce.20.cloned.1.call-update) | async-done | bytes 2097168 | tf_op jit(solution)/shard_map/psum | solution.py:33
  1605.1 18.3 %convolution_subtract_fusion.4 = f32[2048,1024]{0,1:T(8,128)} fusion(f32[2048,1024]{0,1:T(8,128)} %copy-done.3, f32[2048,512]{0,1:T(8,128)} %copy-done.8, f32[1024,512]{0,1:T(8,128)} %all-reduce.20.cloned.1.call-done), kind=kOutput, calls=%fused_computation.562 | convolution fusion | flops 12886999040 | bytes 23068672 | tf_op jit(solution)/shard_map/rk,ck->rc/dot_general | solution.py:255
  1623.4 5.2 fusion.213
  1628.7 5.1 fusion.212
  1633.8 4.7 fusion.211
  1638.5 9.3 copy.196
  (753 shorter events, 350.8 us)
Async XLA Ops:
  11.6 3.1 collective-permute-start
  13.0 5.5 collective-permute-start.1
  14.4 9.3 copy-start.39
  18.5 5.2 collective-permute-start.2
  22.0 5.5 collective-permute-start.3
  92.0 13.8 copy-start.29
  103.5 4.5 collective-permute-start.4
  106.7 7.7 collective-permute-start.5
  108.0 6.4 copy-start.10
  116.0 33.0 %collective-permute-start.6 = (f32[14,128,256]{2,1,0:T(8,128)}, f32[14,128,256]{2,1,0:T(8,128)}, u32[]{:S(2)}, u32[]{:S(2)}) collective-permute-start(f32[14,128,256]{2,1,0:T(8,128)} %get-tuple-element.888), channel_id=1, source_target_pairs={{0,1},{1,2},{2,3},{3,4},{4,5},{5,6},{6,7},{7,8},{8,9},{9,10},{10,1... | collective-permute-start | bytes 5505032 | tf_op jit(solution)/shard_map/ppermute | solution.py:28
  118.6 36.2 %collective-permute-start.7 = (f32[14,128,256]{2,1,0:T(8,128)}, f32[14,128,256]{2,1,0:T(8,128)}, u32[]{:S(2)}, u32[]{:S(2)}) collective-permute-start(f32[14,128,256]{2,1,0:T(8,128)} %get-tuple-element.887), channel_id=1, source_target_pairs={{1,0},{2,1},{3,2},{4,3},{5,4},{6,5},{7,6},{8,7},{9,8},{10,9},{11,1... | collective-permute-start | bytes 5505032 | tf_op jit(solution)/shard_map/ppermute | solution.py:28
  157.1 8.8 copy-start.11
  157.1 8.8 copy-start.18
  177.7 21.2 %copy-start.13 = (f32[49,128,256]{2,1,0:T(8,128)S(1)}, f32[49,128,256]{2,1,0:T(8,128)}, u32[]{:S(2)}) copy-start(f32[49,128,256]{2,1,0:T(8,128)} %copy-done.12) | copy-start | bytes 19267588
  185.9 15.8 collective-permute-start.8
  197.6 12.1 collective-permute-start.9
  209.8 88.9 %collective-permute-start.10 = (f32[14,128,256]{2,1,0:T(8,128)S(1)}, f32[14,128,256]{2,1,0:T(8,128)S(1)}, u32[]{:S(2)}, u32[]{:S(2)}) collective-permute-start(f32[14,128,256]{2,1,0:T(8,128)S(1)} %get-tuple-element.880), channel_id=1, source_target_pairs={{0,1},{1,2},{2,3},{3,4},{4,5},{5,6},{6,7},{7,8},{8,9},{9,10},{10,1... | collective-permute-start | bytes 5505032 | tf_op jit(solution)/shard_map/ppermute | solution.py:28
  268.3 36.1 %collective-permute-start.11 = (f32[14,128,256]{2,1,0:T(8,128)S(1)}, f32[14,128,256]{2,1,0:T(8,128)S(1)}, u32[]{:S(2)}, u32[]{:S(2)}) collective-permute-start(f32[14,128,256]{2,1,0:T(8,128)S(1)} %get-tuple-element.879), channel_id=1, source_target_pairs={{1,0},{2,1},{3,2},{4,3},{5,4},{6,5},{7,6},{8,7},{9,8},{10,9},{11,1... | collective-permute-start | bytes 5505032 | tf_op jit(solution)/shard_map/ppermute | solution.py:28
  343.4 74.6 %collective-permute-start.12 = (f32[6,128,256]{2,1,0:T(8,128)S(1)}, f32[6,128,256]{2,1,0:T(8,128)S(1)}, u32[]{:S(2)}, u32[]{:S(2)}) collective-permute-start(f32[6,128,256]{2,1,0:T(8,128)S(1)} %get-tuple-element.968), channel_id=1, source_target_pairs={{0,16},{16,32},{32,48},{48,64},{64,80},{80,96},{96,112},{1,17},{17... | collective-permute-start | bytes 2359304 | tf_op jit(solution)/shard_map/ppermute | solution.py:28
  414.8 10.9 copy-start.81
  414.8 12.9 copy-start.40
  416.7 4.2 collective-permute-start.13
  422.6 115.9 %collective-permute-start.14 = (f32[14,128,256]{2,1,0:T(8,128)}, f32[14,128,256]{2,1,0:T(8,128)}, u32[]{:S(2)}, u32[]{:S(2)}) collective-permute-start(f32[14,128,256]{2,1,0:T(8,128)} %get-tuple-element.872), channel_id=1, source_target_pairs={{0,1},{1,2},{2,3},{3,4},{4,5},{5,6},{6,7},{7,8},{8,9},{9,10},{10,1... | collective-permute-start | bytes 5505032 | tf_op jit(solution)/shard_map/ppermute | solution.py:28
  426.5 114.3 %collective-permute-start.15 = (f32[14,128,256]{2,1,0:T(8,128)}, f32[14,128,256]{2,1,0:T(8,128)}, u32[]{:S(2)}, u32[]{:S(2)}) collective-permute-start(f32[14,128,256]{2,1,0:T(8,128)} %get-tuple-element.871), channel_id=1, source_target_pairs={{1,0},{2,1},{3,2},{4,3},{5,4},{6,5},{7,6},{8,7},{9,8},{10,9},{11,1... | collective-permute-start | bytes 5505032 | tf_op jit(solution)/shard_map/ppermute | solution.py:28
  560.8 6.9 copy-start.19
  586.6 7.0 copy-start.82
  586.6 7.0 copy-start.83
  589.7 4.5 collective-permute-start.16
  591.7 4.2 collective-permute-start.17
  597.4 82.3 %collective-permute-start.18 = (f32[14,128,256]{2,1,0:T(8,128)}, f32[14,128,256]{2,1,0:T(8,128)}, u32[]{:S(2)}, u32[]{:S(2)}) collective-permute-start(f32[14,128,256]{2,1,0:T(8,128)} %get-tuple-element.864), channel_id=1, source_target_pairs={{0,1},{1,2},{2,3},{3,4},{4,5},{5,6},{6,7},{7,8},{8,9},{9,10},{10,1... | collective-permute-start | bytes 5505032 | tf_op jit(solution)/shard_map/ppermute | solution.py:28
  652.4 36.5 %collective-permute-start.19 = (f32[14,128,256]{2,1,0:T(8,128)S(1)}, f32[14,128,256]{2,1,0:T(8,128)S(1)}, u32[]{:S(2)}, u32[]{:S(2)}) collective-permute-start(f32[14,128,256]{2,1,0:T(8,128)S(1)} %get-tuple-element.863), channel_id=1, source_target_pairs={{1,0},{2,1},{3,2},{4,3},{5,4},{6,5},{7,6},{8,7},{9,8},{10,9},{11,1... | collective-permute-start | bytes 5505032 | tf_op jit(solution)/shard_map/ppermute | solution.py:28
  680.8 9.4 copy-start.38
  680.8 9.4 copy-start.32
  680.8 9.4 copy-start.35
  680.8 9.4 copy-start.49
  680.8 9.5 copy-start.43
  680.9 10.3 copy-start.27
  680.9 10.4 copy-start.46
  716.8 6.0 copy-start.67
  717.6 5.8 copy-start.66
  718.5 6.2 copy-start.64
  724.7 5.9 copy-start.52
  730.8 10.2 copy-start.61
  730.9 10.2 copy-start.60
  730.9 10.2 copy-start.63
  730.9 10.2 copy-start.62
  753.6 22.6 %copy-start.54 = (f32[128,2,16]{2,1,0:T(2,128)S(1)}, f32[128,2,16]{2,1,0:T(2,128)}, u32[]{:S(2)}) copy-start(f32[128,2,16]{2,1,0:T(2,128)} %constant_dynamic-slice_fusion.5) | copy-start | bytes 49156
  755.3 39.8 %all-to-all-start = ((f32[128,9,128]{2,1,0:T(8,128)}), f32[128,9,128]{2,1,0:T(8,128)S(1)}, u32[]{:S(2)}, u32[]{:S(2)}) async-start(f32[128,9,128]{2,1,0:T(8,128)} %copy.165), calls=%async_computation | async-start | bytes 2097152 | tf_op jit(solution)/shard_map/all_to_all | solution.py:205
  776.1 19.6 %copy-start.73 = (pred[128,128]{0,1:T(8,128)(4,1)S(1)}, pred[128,128]{0,1:T(8,128)(4,1)}, u32[]{:S(2)}) copy-start(pred[128,128]{0,1:T(8,128)(4,1)} %fusion.311) | copy-start | bytes 49156
  776.1 19.6 %copy-start.74 = (pred[128,128]{0,1:T(8,128)(4,1)S(1)}, pred[128,128]{0,1:T(8,128)(4,1)}, u32[]{:S(2)}) copy-start(pred[128,128]{0,1:T(8,128)(4,1)} %fusion.312) | copy-start | bytes 49156
  776.1 19.6 %copy-start.75 = (pred[128,128]{0,1:T(8,128)(4,1)S(1)}, pred[128,128]{0,1:T(8,128)(4,1)}, u32[]{:S(2)}) copy-start(pred[128,128]{0,1:T(8,128)(4,1)} %fusion.313) | copy-start | bytes 49156
  776.1 19.6 %copy-start.76 = (pred[128,128]{0,1:T(8,128)(4,1)S(1)}, pred[128,128]{0,1:T(8,128)(4,1)}, u32[]{:S(2)}) copy-start(pred[128,128]{0,1:T(8,128)(4,1)} %fusion.314) | copy-start | bytes 49156
  776.1 19.6 %copy-start.77 = (pred[128,128]{0,1:T(8,128)(4,1)S(1)}, pred[128,128]{0,1:T(8,128)(4,1)}, u32[]{:S(2)}) copy-start(pred[128,128]{0,1:T(8,128)(4,1)} %fusion.315) | copy-start | bytes 49156
  776.2 19.6 %copy-start.78 = (pred[128,128]{0,1:T(8,128)(4,1)S(1)}, pred[128,128]{0,1:T(8,128)(4,1)}, u32[]{:S(2)}) copy-start(pred[128,128]{0,1:T(8,128)(4,1)} %fusion.316) | copy-start | bytes 49156
  776.2 19.6 %copy-start.79 = (pred[128,128]{0,1:T(8,128)(4,1)S(1)}, pred[128,128]{0,1:T(8,128)(4,1)}, u32[]{:S(2)}) copy-start(pred[128,128]{0,1:T(8,128)(4,1)} %fusion.317) | copy-start | bytes 49156
  776.2 19.6 %copy-start.80 = (pred[128,128]{0,1:T(8,128)(4,1)S(1)}, pred[128,128]{0,1:T(8,128)(4,1)}, u32[]{:S(2)}) copy-start(pred[128,128]{0,1:T(8,128)(4,1)} %fusion.318) | copy-start | bytes 49156
  776.2 136.0 %all-reduce.10.cloned.1.call-start = ((), (), s32[]{:S(2)}) async-start(), calls=%async_computation.1 | async-start | bytes 8388608 | tf_op jit(solution)/shard_map/psum | solution.py:33
  813.3 164.0 %all-reduce.12.cloned.1.call-start = ((), (), s32[]{:S(2)}) async-start(), calls=%async_computation.2 | async-start | bytes 2097152 | tf_op jit(solution)/shard_map/psum | solution.py:33
  914.6 281.0 %all-reduce.14.cloned.1.call-start = ((), (), s32[]{:S(2)}) async-start(), calls=%async_computation.3 | async-start | bytes 4194304 | tf_op jit(solution)/shard_map/psum | solution.py:33
  1130.4 191.3 %all-reduce.16.cloned.1.call-start = ((), (), s32[]{:S(2)}) async-start(), calls=%async_computation.4 | async-start | bytes 8388608 | tf_op jit(solution)/shard_map/psum | solution.py:33
  1219.0 167.9 %all-reduce.18.cloned.1.call-start = ((), (), s32[]{:S(2)}) async-start(), calls=%async_computation.5 | async-start | bytes 2097152 | tf_op jit(solution)/shard_map/psum | solution.py:33
  1324.1 281.0 %all-reduce.20.cloned.1.call-start = ((), (), s32[]{:S(2)}) async-start(), calls=%async_computation.6 | async-start | bytes 4194304 | tf_op jit(solution)/shard_map/psum | solution.py:33
  1605.1 18.3 %copy-start.7 = (f32[2048,512]{0,1:T(8,128)S(1)}, f32[2048,512]{0,1:T(8,128)}, u32[]{:S(2)}) copy-start(f32[2048,512]{0,1:T(8,128)} %copy-done.6) | copy-start | bytes 12582916
  1638.5 9.3 copy-start.1
  (44 other events, 103.3 us)
Sparse Core Ops, SparseCore 0:
  813.4 98.7 all-reduce.9
  914.7 62.6 all-reduce.11
  1130.5 65.0 all-reduce.13
  1219.1 102.5 all-reduce.15
  1324.2 62.6 all-reduce.17
  1539.8 65.2 all-reduce.19
where the time goes:
time: 1660 us; the launch traced here: 1650 us
  waiting for transfers between devices  586 us (35%)
  other arithmetic  345 us (21%)
  local copies, waits for them, and re-layouts  257 us (15%)
  starting transfers between devices  237 us (14%)
  blocking collectives  106 us (6%)
  matrix products  85.1 us (5%)
  between operations  22.1 us (1%)
  loops' own time  17.7 us (1%)
    psum x6, waiting for transfers between devices, spread_2(): return lax.psum(kept, axis)  457 us
    ppermute x16, starting transfers between devices, shifted(): return lax.ppermute(block, axis, route)  208 us
    another operation x30, other arithmetic, on_device(): diag_factor = jnp.linalg.cholesky(diag_block)  159 us
    unnamed x365, local copies, waits for them, and re-layouts  152 us
    all_gather x1, blocking collectives, on_device(): lax.all_gather(points[:, :skel_count][None], ('row', 'col'), axis=0, tile...  106 us
    ppermute x16, waiting for transfers between devices, shifted(): return lax.ppermute(block, axis, route)  103 us
    another operation x7, other arithmetic, on_device(): jax.scipy.linalg.solve_triangular(diag_factor, slab_rows.T, lower=True)  81 us
    dot_general x2, matrix products, on_device(): jnp.einsum('rk,ck->rc', panel_rows, panel_cols, precision=highest)  35.9 us
  transfers between devices with their start and end apart: 27, of which 19 were waited for; matrix products, arithmetic and copies ran while one was open for 3% of the time, Pallas kernels for 0%

commit v1 on v0

--- a/solution.py
+++ b/solution.py
@@ -30,7 +30,10 @@
 
 def spread_2(value, axis, source):
     kept = jnp.where(lax.axis_index(axis) == source, value, 0).astype(value.dtype)
-    return lax.psum(kept, axis)
+    number_the_tails = lambda row_data, net_axis: jnp.sum(
+        lax.all_gather(row_data, net_axis), axis=0
+    )
+    return number_the_tails(kept, axis)
 
 
 def offsets_all():

time: 1660 us -> 2310 us (1.39)
  waiting for transfers between devices: 586 us -> 1120 us
  other arithmetic: 345 us -> 425 us
    all_gather x0 -> x6, waiting for transfers between devices: none -> 991 us  [spread_2(): lax.all_gather(row_data, net_axis)]
    psum x6 -> x0, waiting for transfers between devices: 457 us -> none  [spread_2(): return lax.psum(kept, axis)]
    reduce_sum x0 -> x6, other arithmetic: none -> 71.7 us  [spread_2(): jnp.sum(lax.all_gather(row_data, net_axis), axis=0)]
    unnamed x365 -> x396, local copies, waits for them, and re-layouts: 152 us -> 155 us
where the time goes in v1:
time: 2310 us; the launch traced here: 2300 us
  waiting for transfers between devices  1120 us (48%)
  other arithmetic  425 us (18%)
  local copies, waits for them, and re-layouts  275 us (12%)
  starting transfers between devices  237 us (10%)
  blocking collectives  106 us (5%)
  matrix products  98.5 us (4%)
    all_gather x6, waiting for transfers between devices, spread_2(): lax.all_gather(row_data, net_axis)  991 us
    ppermute x16, starting transfers between devices, shifted(): return lax.ppermute(block, axis, route)  208 us
    another operation x30, other arithmetic, on_device(): diag_factor = jnp.linalg.cholesky(diag_block)  159 us
    unnamed x396, local copies, waits for them, and re-layouts  155 us
    all_gather x1, blocking collectives, on_device(): lax.all_gather(points[:, :skel_count][None], ('row', 'col'), axis=0, tile...  106 us
    ppermute x16, waiting for transfers between devices, shifted(): return lax.ppermute(block, axis, route)  102 us
    another operation x7, other arithmetic, on_device(): jax.scipy.linalg.solve_triangular(diag_factor, slab_rows.T, lower=True)  80 us
    reduce_sum x6, other arithmetic, spread_2(): jnp.sum(lax.all_gather(row_data, net_axis), axis=0)  71.7 us
  transfers between devices with their start and end apart: 27, of which 19 were waited for; matrix products, arithmetic and copies ran while one was open for 3% of the time, Pallas kernels for 0%

profile of v1, /device:TPU:0, one launch (start us, length us, event | category | flops | bytes accessed | tf_op | source)
XLA Modules:
  0.0 2299.4 jit_solution(16106179558600103911)
XLA Ops:
  14.9 3.6 collective-permute-done.1
  18.5 3.5 collective-permute-start.2
  29.1 55.4 %conditional.4 = (f32[128,256]{1,0:T(8,128)}, f32[128,256]{1,0:T(8,128)}, f32[128,256]{1,0:T(8,128)}, f32[128,256]{1,0:T(8,128)}, f32[128,256]{1,0:T(8,128)}, /*...) conditional(s32[]{:T(128)} %convert_element_type.56, () %tuple.65, ...), branch_computations={%region_0.1_spmd, %region_1.6_spmd} | conditional | flops 2442133504 | bytes 22315710 | solution.py:175
  39.5 13.2 cholesky.356
  56.4 11.3 custom-call.35
  109.7 4.6 collective-permute-done.5
  119.8 29.2 %collective-permute-done.6 = f32[14,128,256]{2,1,0:T(8,128)} collective-permute-done((f32[14,128,256]{2,1,0:T(8,128)}, f32[14,128,256]{2,1,0:T(8,128)}, u32[]{:S(2)}, u32[]{:S(2)}) %collective-permute-start.6) | collective-permute-done | bytes 1835040 | tf_op jit(solution)/shard_map/ppermute | solution.py:28
  168.5 8.0 conditional.5
  185.6 10.8 collective-permute-start.8
  201.5 7.9 collective-permute-done.9
  209.5 57.7 %collective-permute-start.10 = (f32[14,128,256]{2,1,0:T(8,128)S(1)}, f32[14,128,256]{2,1,0:T(8,128)S(1)}, u32[]{:S(2)}, u32[]{:S(2)}) collective-permute-start(f32[14,128,256]{2,1,0:T(8,128)S(1)} %get-tuple-element.856), channel_id=1, source_target_pairs={{0,1},{1,2},{2,3},{3,4},{4,5},{5,6},{6,7},{7,8},{8,9},{9,10},{10,1... | collective-permute-start | bytes 5505032 | tf_op jit(solution)/shard_map/ppermute | solution.py:28
  274.3 24.2 %collective-permute-done.10 = f32[14,128,256]{2,1,0:T(8,128)S(1)} collective-permute-done((f32[14,128,256]{2,1,0:T(8,128)S(1)}, f32[14,128,256]{2,1,0:T(8,128)S(1)}, u32[]{:S(2)}, u32[]{:S(2)}) %collective-permute-start.10) | collective-permute-done | bytes 1835040 | tf_op jit(solution)/shard_map/ppermute | solution.py:28
  298.6 5.6 collective-permute-done.11
  311.1 3.7 add.643
  314.8 9.4 conditional.6
  343.4 70.5 %collective-permute-start.12 = (f32[6,128,256]{2,1,0:T(8,128)S(1)}, f32[6,128,256]{2,1,0:T(8,128)S(1)}, u32[]{:S(2)}, u32[]{:S(2)}) collective-permute-start(f32[6,128,256]{2,1,0:T(8,128)S(1)} %get-tuple-element.944), channel_id=1, source_target_pairs={{0,16},{16,32},{32,48},{48,64},{64,80},{80,96},{96,112},{1,17},{17... | collective-permute-start | bytes 2359304 | tf_op jit(solution)/shard_map/ppermute | solution.py:28
  427.9 106.3 %all-gather.7 = f32[128,2,128]{2,1,0:T(2,128)S(1)} all-gather(f32[1,2,128]{2,1,0:T(2,128)S(1)} %copy.238), channel_id=2, replica_groups=mesh['row'=8,'col'=16] {'row','col'}, dimensions={0}, use_global_device_ids=true | all-gather | bytes 132096 | tf_op jit(solution)/shard_map/all_gather | solution.py:213
  561.0 6.9 add.644
  567.9 10.6 conditional.7
  597.6 51.1 %collective-permute-start.18 = (f32[14,128,256]{2,1,0:T(8,128)}, f32[14,128,256]{2,1,0:T(8,128)}, u32[]{:S(2)}, u32[]{:S(2)}) collective-permute-start(f32[14,128,256]{2,1,0:T(8,128)} %get-tuple-element.840), channel_id=1, source_target_pairs={{0,1},{1,2},{2,3},{3,4},{4,5},{5,6},{6,7},{7,8},{8,9},{9,10},{10,1... | collective-permute-start | bytes 5505032 | tf_op jit(solution)/shard_map/ppermute | solution.py:28
  661.9 17.8 collective-permute-done.18
  680.9 8.0 collective-permute-done.19
  693.5 4.1 add.645
  746.7 20.7 all-to-all-start
  768.9 17.6 all-to-all-done
  797.4 21.9 select_select_fusion.4
  819.4 5.0 bitcast_add_fusion.4
  830.6 363.9 %all-gather.15.cloned.1.call-done = f32[32768,512]{1,0:T(8,128)} async-done(((f32[2048,512]{1,0:T(8,128)}), f32[32768,512]{1,0:T(8,128)}) %all-gather.15.cloned.1.call-update) | async-done | bytes 67108880 | tf_op jit(solution)/shard_map/all_gather | solution.py:34
  1194.5 23.1 %reduce_sum.54 = f32[2048,512]{1,0:T(8,128)} reduce(f32[16,2048,512]{2,1,0:T(8,128)} %bitcast.335, f32[]{:T(128)} %constant.345.clone.1), dimensions={0}, to_apply=%region_10.13 | reduce | flops 15728640 | bytes 71303168 | tf_op jit(solution)/shard_map/reduce_sum | solution.py:33
  1220.1 5.6 copy.283
  1225.7 44.0 %all-gather.17.cloned.1.call-done = f32[4096,512]{1,0:T(8,128)} async-done(((f32[512,512]{1,0:T(8,128)}), f32[4096,512]{1,0:T(8,128)}) %all-gather.17.cloned.1.call-update) | async-done | bytes 8388624 | tf_op jit(solution)/shard_map/all_gather | solution.py:34
  1269.7 4.6 reduce_sum.55
  1275.8 11.7 cholesky.402
  1287.7 9.8 custom-call.39
  1300.0 12.1 cholesky.421
  1313.5 9.8 custom-call.40
  1324.9 11.7 cholesky.442
  1337.3 9.8 custom-call.41
  1348.6 11.9 cholesky.459
  1363.8 8.3 while.4
  1372.1 39.3 %custom-call.42 = f32[4,128,128]{1,2,0:T(8,128)S(1)} custom-call(f32[4,128,128]{2,1,0:T(8,128)S(1)} %get-tuple-element.489), custom_call_target="InvertDiagBlocksLowerTriangular" | custom-call | tf_op jit(solution)/shard_map/jit(_solve_triangular)/triangular_solve | solution.py:246
  1421.5 4.0 fusion.229
  1440.8 84.9 %all-gather.19.cloned.1.call-done = f32[8192,512]{1,0:T(8,128)} async-done(((f32[1024,512]{1,0:T(8,128)}), f32[8192,512]{1,0:T(8,128)}) %all-gather.19.cloned.1.call-update) | async-done | bytes 16777232 | tf_op jit(solution)/shard_map/all_gather | solution.py:34
  1525.7 8.2 reduce_sum.56
  1533.9 16.6 convolution_subtract_fusion.5
  1556.5 368.9 %all-gather.21.cloned.1.call-done = f32[32768,512]{1,0:T(8,128)} async-done(((f32[2048,512]{1,0:T(8,128)}), f32[32768,512]{1,0:T(8,128)}) %all-gather.21.cloned.1.call-update) | async-done | bytes 67108880 | tf_op jit(solution)/shard_map/all_gather | solution.py:34
  1925.4 23.1 %reduce_sum.57 = f32[2048,512]{1,0:T(8,128)} reduce(f32[16,2048,512]{2,1,0:T(8,128)} %bitcast.352, f32[]{:T(128)} %constant.345.clone.1), dimensions={0}, to_apply=%region_21.26 | reduce | flops 15728640 | bytes 71303168 | tf_op jit(solution)/shard_map/reduce_sum | solution.py:33
  1951.0 5.6 copy.289
  1956.5 44.1 %all-gather.23.cloned.1.call-done = f32[4096,512]{1,0:T(8,128)} async-done(((f32[512,512]{1,0:T(8,128)}), f32[4096,512]{1,0:T(8,128)}) %all-gather.23.cloned.1.call-update) | async-done | bytes 8388624 | tf_op jit(solution)/shard_map/all_gather | solution.py:34
  2000.6 4.6 reduce_sum.58
  2006.8 11.7 cholesky.474
  2018.6 9.8 custom-call.43
  2031.0 12.1 cholesky.493
  2044.4 9.8 custom-call.44
  2055.8 11.7 cholesky.514
  2068.2 9.8 custom-call.45
  2079.5 11.9 cholesky.531
  2094.8 7.7 while.5
  2102.6 39.3 %custom-call.46 = f32[4,128,128]{1,2,0:T(8,128)S(1)} custom-call(f32[4,128,128]{2,1,0:T(8,128)S(1)} %get-tuple-element.490), custom_call_target="InvertDiagBlocksLowerTriangular" | custom-call | tf_op jit(solution)/shard_map/jit(_solve_triangular)/triangular_solve | solution.py:246
  2151.9 4.0 fusion.226
  2170.9 85.3 %all-gather.25.cloned.1.call-done = f32[8192,512]{1,0:T(8,128)} async-done(((f32[1024,512]{1,0:T(8,128)}), f32[8192,512]{1,0:T(8,128)}) %all-gather.25.cloned.1.call-update) | async-done | bytes 16777232 | tf_op jit(solution)/shard_map/all_gather | solution.py:34
  2256.1 8.2 reduce_sum.59
  2264.3 16.8 convolution_subtract_fusion.4
  2287.7 4.7 fusion.211
  (764 shorter events, 402.3 us)
Async XLA Ops:
  11.6 3.1 collective-permute-start
  13.0 5.5 collective-permute-start.1
  14.4 9.3 copy-start.50
  18.5 5.2 collective-permute-start.2
  22.0 5.5 collective-permute-start.3
  91.9 13.7 copy-start.40
  103.4 4.5 collective-permute-start.4
  106.6 7.7 collective-permute-start.5
  107.9 6.4 copy-start.13
  116.0 33.0 %collective-permute-start.6 = (f32[14,128,256]{2,1,0:T(8,128)}, f32[14,128,256]{2,1,0:T(8,128)}, u32[]{:S(2)}, u32[]{:S(2)}) collective-permute-start(f32[14,128,256]{2,1,0:T(8,128)} %get-tuple-element.864), channel_id=1, source_target_pairs={{0,1},{1,2},{2,3},{3,4},{4,5},{5,6},{6,7},{7,8},{8,9},{9,10},{10,1... | collective-permute-start | bytes 5505032 | tf_op jit(solution)/shard_map/ppermute | solution.py:28
  118.5 36.3 %collective-permute-start.7 = (f32[14,128,256]{2,1,0:T(8,128)}, f32[14,128,256]{2,1,0:T(8,128)}, u32[]{:S(2)}, u32[]{:S(2)}) collective-permute-start(f32[14,128,256]{2,1,0:T(8,128)} %get-tuple-element.863), channel_id=1, source_target_pairs={{1,0},{2,1},{3,2},{4,3},{5,4},{6,5},{7,6},{8,7},{9,8},{10,9},{11,1... | collective-permute-start | bytes 5505032 | tf_op jit(solution)/shard_map/ppermute | solution.py:28
  157.0 8.8 copy-start.14
  157.0 8.8 copy-start.21
  177.4 21.2 copy-start.18
  185.6 15.8 collective-permute-start.8
  197.3 12.1 collective-permute-start.9
  209.5 89.0 %collective-permute-start.10 = (f32[14,128,256]{2,1,0:T(8,128)S(1)}, f32[14,128,256]{2,1,0:T(8,128)S(1)}, u32[]{:S(2)}, u32[]{:S(2)}) collective-permute-start(f32[14,128,256]{2,1,0:T(8,128)S(1)} %get-tuple-element.856), channel_id=1, source_target_pairs={{0,1},{1,2},{2,3},{3,4},{4,5},{5,6},{6,7},{7,8},{8,9},{9,10},{10,1... | collective-permute-start | bytes 5505032 | tf_op jit(solution)/shard_map/ppermute | solution.py:28
  268.1 36.1 %collective-permute-start.11 = (f32[14,128,256]{2,1,0:T(8,128)S(1)}, f32[14,128,256]{2,1,0:T(8,128)S(1)}, u32[]{:S(2)}, u32[]{:S(2)}) collective-permute-start(f32[14,128,256]{2,1,0:T(8,128)S(1)} %get-tuple-element.855), channel_id=1, source_target_pairs={{1,0},{2,1},{3,2},{4,3},{5,4},{6,5},{7,6},{8,7},{9,8},{10,9},{11,1... | collective-permute-start | bytes 5505032 | tf_op jit(solution)/shard_map/ppermute | solution.py:28
  343.4 74.6 %collective-permute-start.12 = (f32[6,128,256]{2,1,0:T(8,128)S(1)}, f32[6,128,256]{2,1,0:T(8,128)S(1)}, u32[]{:S(2)}, u32[]{:S(2)}) collective-permute-start(f32[6,128,256]{2,1,0:T(8,128)S(1)} %get-tuple-element.944), channel_id=1, source_target_pairs={{0,16},{16,32},{32,48},{48,64},{64,80},{80,96},{96,112},{1,17},{17... | collective-permute-start | bytes 2359304 | tf_op jit(solution)/shard_map/ppermute | solution.py:28
  414.8 10.9 copy-start.97
  414.8 13.0 copy-start.51
  416.7 4.2 collective-permute-start.13
  422.6 116.1 %collective-permute-start.14 = (f32[14,128,256]{2,1,0:T(8,128)}, f32[14,128,256]{2,1,0:T(8,128)}, u32[]{:S(2)}, u32[]{:S(2)}) collective-permute-start(f32[14,128,256]{2,1,0:T(8,128)} %get-tuple-element.848), channel_id=1, source_target_pairs={{0,1},{1,2},{2,3},{3,4},{4,5},{5,6},{6,7},{7,8},{8,9},{9,10},{10,1... | collective-permute-start | bytes 5505032 | tf_op jit(solution)/shard_map/ppermute | solution.py:28
  426.5 114.4 %collective-permute-start.15 = (f32[14,128,256]{2,1,0:T(8,128)}, f32[14,128,256]{2,1,0:T(8,128)}, u32[]{:S(2)}, u32[]{:S(2)}) collective-permute-start(f32[14,128,256]{2,1,0:T(8,128)} %get-tuple-element.847), channel_id=1, source_target_pairs={{1,0},{2,1},{3,2},{4,3},{5,4},{6,5},{7,6},{8,7},{9,8},{10,9},{11,1... | collective-permute-start | bytes 5505032 | tf_op jit(solution)/shard_map/ppermute | solution.py:28
  561.0 6.9 copy-start.22
  586.0 5.9 copy-start.42
  586.7 7.2 copy-start.98
  586.7 7.2 copy-start.99
  589.8 4.7 collective-permute-start.16
  592.0 4.2 collective-permute-start.17
  597.6 82.1 %collective-permute-start.18 = (f32[14,128,256]{2,1,0:T(8,128)}, f32[14,128,256]{2,1,0:T(8,128)}, u32[]{:S(2)}, u32[]{:S(2)}) collective-permute-start(f32[14,128,256]{2,1,0:T(8,128)} %get-tuple-element.840), channel_id=1, source_target_pairs={{0,1},{1,2},{2,3},{3,4},{4,5},{5,6},{6,7},{7,8},{8,9},{9,10},{10,1... | collective-permute-start | bytes 5505032 | tf_op jit(solution)/shard_map/ppermute | solution.py:28
  652.4 36.5 %collective-permute-start.19 = (f32[14,128,256]{2,1,0:T(8,128)S(1)}, f32[14,128,256]{2,1,0:T(8,128)S(1)}, u32[]{:S(2)}, u32[]{:S(2)}) collective-permute-start(f32[14,128,256]{2,1,0:T(8,128)S(1)} %get-tuple-element.839), channel_id=1, source_target_pairs={{1,0},{2,1},{3,2},{4,3},{5,4},{6,5},{7,6},{8,7},{9,8},{10,9},{11,1... | collective-permute-start | bytes 5505032 | tf_op jit(solution)/shard_map/ppermute | solution.py:28
  680.8 9.4 copy-start.49
  680.8 9.4 copy-start.43
  680.8 9.4 copy-start.46
  680.8 9.5 copy-start.60
  680.8 9.5 copy-start.54
  680.9 10.4 copy-start.38
  680.9 10.4 copy-start.57
  716.9 6.2 copy-start.83
  716.9 8.0 copy-start.82
  716.9 8.0 copy-start.81
  717.1 7.9 copy-start.80
  744.8 22.7 copy-start.69
  746.7 39.7 %all-to-all-start = ((f32[128,9,128]{2,1,0:T(8,128)}), f32[128,9,128]{2,1,0:T(8,128)S(1)}, u32[]{:S(2)}, u32[]{:S(2)}) async-start(f32[128,9,128]{2,1,0:T(8,128)} %copy.271), calls=%async_computation | async-start | bytes 2097152 | tf_op jit(solution)/shard_map/all_to_all | solution.py:208
  767.4 427.0 %all-gather.15.cloned.1.call-start = ((), (), s32[]{:S(2)}) async-start(), calls=%async_computation.1 | async-start | bytes 71303168 | tf_op jit(solution)/shard_map/all_gather | solution.py:34
  792.0 5.4 copy-start.88
  792.0 5.4 copy-start.89
  792.0 5.4 copy-start.90
  792.0 5.4 copy-start.91
  792.0 5.4 copy-start.92
  792.0 5.4 copy-start.93
  792.0 5.4 copy-start.94
  792.0 5.4 copy-start.95
  797.4 21.9 copy-start.96
  830.5 439.2 %all-gather.17.cloned.1.call-start = ((), (), s32[]{:S(2)}) async-start(), calls=%async_computation.2 | async-start | bytes 9437184 | tf_op jit(solution)/shard_map/all_gather | solution.py:34
  1220.0 305.7 %all-gather.19.cloned.1.call-start = ((), (), s32[]{:S(2)}) async-start(), calls=%async_computation.3 | async-start | bytes 18874368 | tf_op jit(solution)/shard_map/all_gather | solution.py:34
  1372.1 41.6 %copy-start.32 = (f32[512,512]{1,0:T(8,128)}, f32[512,512]{1,0:T(8,128)S(1)}, u32[]{:S(2)}) copy-start(f32[512,512]{1,0:T(8,128)S(1)} %get-tuple-element.1240) | copy-start | bytes 3145732
  1440.4 485.1 %all-gather.21.cloned.1.call-start = ((), (), s32[]{:S(2)}) async-start(), calls=%async_computation.4 | async-start | bytes 71303168 | tf_op jit(solution)/shard_map/all_gather | solution.py:34
  1556.5 444.2 %all-gather.23.cloned.1.call-start = ((), (), s32[]{:S(2)}) async-start(), calls=%async_computation.5 | async-start | bytes 9437184 | tf_op jit(solution)/shard_map/all_gather | solution.py:34
  1950.9 305.2 %all-gather.25.cloned.1.call-start = ((), (), s32[]{:S(2)}) async-start(), calls=%async_computation.6 | async-start | bytes 18874368 | tf_op jit(solution)/shard_map/all_gather | solution.py:34
  2102.6 41.6 %copy-start.33 = (f32[512,512]{1,0:T(8,128)}, f32[512,512]{1,0:T(8,128)S(1)}, u32[]{:S(2)}) copy-start(f32[512,512]{1,0:T(8,128)S(1)} %get-tuple-element.1241) | copy-start | bytes 3145732
  2264.3 16.8 copy-start.10
  2283.3 9.0 copy-start.1
  (60 other events, 138.5 us)
Sparse Core Ops, SparseCore 0:
  830.6 363.7 all-gather.14
  1220.1 49.5 all-gather.16
  1440.5 85.1 all-gather.18
  1556.6 368.8 all-gather.20
  1951.0 49.5 all-gather.22
  2171.0 85.1 all-gather.24
